TPU v7x, 32 devices: a whole 2x2x4 slice. The times are simulated.
32 devices in a mesh: batch: 8 (over z, y), seq: 4 (over x, core).
Axes of the slice: x: 2, y: 2, z: 4, core: 2. Of those that a mesh axis runs over, the one named last changes fastest.
Arguments:
- inputs: bfloat16 [16, 1024, 768], P('batch', 'seq'), may hold values from -6 to 6
- segments: int32 [16, 1024], P('batch'), may hold values from 0 to 7, never falling along the last dimension, each value on 1 to 512 neighbouring positions
- qkv_weight: bfloat16 [768, 2304], replicated, may hold values from -0.21875 to 0.21875
- query_bias: bfloat16 [768], replicated, may hold values from -3 to 3
- value_bias: bfloat16 [768], replicated, may hold values from -3 to 3
- out_weight: bfloat16 [768, 768], replicated, may hold values from -1.75 to 1.75
- out_bias: bfloat16 [768], replicated, may hold values from -3 to 3
- norm1_gain: bfloat16 [768], replicated, may hold values from 0.099609375 to 1.8984375
- norm1_shift: bfloat16 [768], replicated, may hold values from -3 to 3
- up_weight: bfloat16 [768, 3072], replicated, may hold values from -0.21875 to 0.21875
- up_bias: bfloat16 [3072], replicated, may hold values from -3 to 3
- down_weight: bfloat16 [3072, 768], replicated, may hold values from -0.109375 to 0.109375
- down_bias: bfloat16 [768], replicated, may hold values from -3 to 3
- norm2_gain: bfloat16 [768], replicated, may hold values from 0.099609375 to 1.8984375
- norm2_shift: bfloat16 [768], replicated, may hold values from -3 to 3
- cotangent: bfloat16 [16, 1024, 768], P('batch', 'seq'), may hold values from -6 to 6
Outputs:
- outputs: bfloat16 [16, 1024, 768], P('batch', 'seq')
- input_grad: float32 [16, 1024, 768], P('batch', 'seq')
- qkv_weight_grad: float32 [768, 2304], P('batch', 'seq')
- query_bias_grad: float32 [768], replicated
- value_bias_grad: float32 [768], replicated
- out_weight_grad: float32 [768, 768], P('batch', 'seq')
- out_bias_grad: float32 [768], replicated
- norm1_gain_grad: float32 [768], replicated
- norm1_shift_grad: float32 [768], replicated
- up_weight_grad: float32 [768, 3072], P('batch', 'seq')
- up_bias_grad: float32 [3072], replicated
- down_weight_grad: float32 [3072, 768], P('batch', 'seq')
- down_bias_grad: float32 [768], replicated
- norm2_gain_grad: float32 [768], replicated
- norm2_shift_grad: float32 [768], replicated
Inputs may be any that keep to these rules, and one draw needn't show every extreme that they name: `segments`: in each packed row the passage numbers never fall, every number below 8 occurs, each passage holds 1 to 512 positions, and one passage in each row holds exactly 512.
All inputs are finite; a program needn't handle non-finite values.
Results may differ from a plain program's by a relative error of at most 0.013.
The roundings to bfloat16 on the way count: a program that leaves them out, or rounds other values in their place, can miss the bound.
Values may be sent and summed in bfloat16 or wider, within the bound.
No kernel may reach another device: no remote copies, remote signals or barrier semaphores. Data moves between devices by JAX's collectives and lax.ppermute only.
A program may use at most 192 MiB of HBM per device.

v0:
```python
import jax
import jax.numpy as jnp
from jax import lax
from jax.sharding import PartitionSpec as P

DH = 64
EPS = 1e-05
NEG = -1000000000.0


def layer_norm(values, gain, shift):
    mean = jnp.mean(values, axis=-1, keepdims=True)
    centred = values - mean
    spread = jnp.mean(centred * centred, axis=-1, keepdims=True)
    return centred * lax.rsqrt(spread + EPS) * gain + shift


def gelu_exact(values):
    return jax.nn.gelu(values, approximate=False)


def row_scores(query, keys, segment):
    scores = jnp.einsum("qhd,khd->hqk", query, keys, preferred_element_type=jnp.float32) * DH ** (
        -0.5
    )
    same = segment[:, None] == segment[None, :]
    return jnp.where(same[None], scores, NEG)


def attend_row(parts):
    query, keys, values, segment = parts
    scores = row_scores(query, keys, segment)
    top = jnp.max(scores, axis=-1, keepdims=True)
    expo = jnp.exp(scores - top)
    total = jnp.sum(expo, axis=-1, keepdims=True)
    probs = (expo / total).astype(jnp.bfloat16)
    context = jnp.einsum("hqk,khd->qhd", probs, values, preferred_element_type=jnp.float32)
    return (context.astype(jnp.bfloat16), (top + jnp.log(total))[..., 0])


def attend_back(parts):
    query, keys, values, segment, logsum, d_context = parts
    scores = row_scores(query, keys, segment)
    probs = jnp.exp(scores - logsum[..., None])
    d_values = jnp.einsum(
        "hqk,qhd->khd", probs.astype(jnp.bfloat16), d_context, preferred_element_type=jnp.float32
    )
    d_probs = jnp.einsum("qhd,khd->hqk", d_context, values, preferred_element_type=jnp.float32)
    delta = jnp.sum(probs * d_probs, axis=-1, keepdims=True)
    d_scores = (probs * (d_probs - delta)).astype(jnp.bfloat16)
    d_query = jnp.einsum(
        "hqk,khd->qhd", d_scores, keys, preferred_element_type=jnp.float32
    ) * DH ** (-0.5)
    d_keys = jnp.einsum(
        "hqk,qhd->khd", d_scores, query, preferred_element_type=jnp.float32
    ) * DH ** (-0.5)
    return jnp.stack([d_query, d_keys, d_values], axis=1).astype(jnp.bfloat16)


def body(
    inputs,
    segments,
    qkv_weight,
    query_bias,
    value_bias,
    out_weight,
    out_bias,
    norm1_gain,
    norm1_shift,
    up_weight,
    up_bias,
    down_weight,
    down_bias,
    norm2_gain,
    norm2_shift,
    cotangent,
):
    rows, local_len, width = inputs.shape
    count = rows * local_len
    flat_in = inputs.reshape(count, width)
    qkv_shift = jnp.concatenate(
        [
            query_bias.astype(jnp.float32),
            jnp.zeros((width,), jnp.float32),
            value_bias.astype(jnp.float32),
        ]
    )
    projected = (
        jnp.dot(flat_in, qkv_weight, preferred_element_type=jnp.float32) + qkv_shift
    ).astype(jnp.bfloat16)
    heads_in = lax.all_to_all(
        projected.reshape(rows, local_len, 3, width), "seq", split_axis=3, concat_axis=1, tiled=True
    )
    full_len = heads_in.shape[1]
    per_head = heads_in.shape[3] // DH
    split = heads_in.reshape(rows, full_len, 3, per_head, DH)
    query = split[:, :, 0]
    keys = split[:, :, 1]
    values = split[:, :, 2]
    context, logsum = lax.map(attend_row, (query, keys, values, segments))
    context = context.reshape(rows, full_len, per_head * DH)
    regrouped = lax.all_to_all(context, "seq", split_axis=1, concat_axis=2, tiled=True)
    flat_ctx = regrouped.reshape(count, width)
    attn = jnp.dot(flat_ctx, out_weight, preferred_element_type=jnp.float32) + out_bias.astype(
        jnp.float32
    )
    summed = flat_in.astype(jnp.float32) + attn
    hidden, norm1_back = jax.vjp(
        layer_norm, summed, norm1_gain.astype(jnp.float32), norm1_shift.astype(jnp.float32)
    )
    hidden_low = hidden.astype(jnp.bfloat16)
    pre_act = jnp.dot(hidden_low, up_weight, preferred_element_type=jnp.float32) + up_bias.astype(
        jnp.float32
    )
    act, gelu_back = jax.vjp(gelu_exact, pre_act)
    act_low = act.astype(jnp.bfloat16)
    branch = jnp.dot(act_low, down_weight, preferred_element_type=jnp.float32) + down_bias.astype(
        jnp.float32
    )
    final, norm2_back = jax.vjp(
        layer_norm, hidden + branch, norm2_gain.astype(jnp.float32), norm2_shift.astype(jnp.float32)
    )
    outputs = final.astype(jnp.bfloat16).reshape(rows, local_len, width)
    d_final = cotangent.reshape(count, width).astype(jnp.float32)
    d_res_two, d_gain_two, d_shift_two = norm2_back(d_final)
    d_down_bias = jnp.sum(d_res_two, axis=0)
    d_branch = d_res_two.astype(jnp.bfloat16)
    d_down = jnp.einsum("ti,to->io", act_low, d_branch, preferred_element_type=jnp.float32)
    d_act = jnp.einsum("to,io->ti", d_branch, down_weight, preferred_element_type=jnp.float32)
    (d_pre,) = gelu_back(d_act)
    d_pre_low = d_pre.astype(jnp.bfloat16)
    d_up_bias = jnp.sum(d_pre_low.astype(jnp.float32), axis=0)
    d_up = jnp.einsum("ti,to->io", hidden_low, d_pre_low, preferred_element_type=jnp.float32)
    d_hidden = d_res_two + jnp.einsum(
        "to,io->ti", d_pre_low, up_weight, preferred_element_type=jnp.float32
    )
    d_summed, d_gain_one, d_shift_one = norm1_back(d_hidden)
    d_out_bias = jnp.sum(d_summed, axis=0)
    d_attn = d_summed.astype(jnp.bfloat16)
    d_out = jnp.einsum("ti,to->io", flat_ctx, d_attn, preferred_element_type=jnp.float32)
    d_context = jnp.einsum(
        "to,io->ti", d_attn, out_weight, preferred_element_type=jnp.float32
    ).astype(jnp.bfloat16)
    d_heads = lax.all_to_all(
        d_context.reshape(rows, local_len, width), "seq", split_axis=2, concat_axis=1, tiled=True
    )
    d_heads = d_heads.reshape(rows, full_len, per_head, DH)
    d_split = lax.map(attend_back, (query, keys, values, segments, logsum, d_heads))
    d_back = lax.all_to_all(
        d_split.reshape(rows, full_len, 3, per_head * DH),
        "seq",
        split_axis=1,
        concat_axis=3,
        tiled=True,
    )
    d_proj = d_back.reshape(count, 3 * width)
    d_query_bias = jnp.sum(d_proj[:, :width].astype(jnp.float32), axis=0)
    d_value_bias = jnp.sum(d_proj[:, 2 * width :].astype(jnp.float32), axis=0)
    d_qkv = jnp.einsum("ti,to->io", flat_in, d_proj, preferred_element_type=jnp.float32)
    d_inputs = d_summed + jnp.einsum(
        "to,io->ti", d_proj, qkv_weight, preferred_element_type=jnp.float32
    )
    mats_part = (
        lax.psum_scatter(d_qkv, "seq", scatter_dimension=1, tiled=True),
        lax.psum_scatter(d_out, "seq", scatter_dimension=1, tiled=True),
        lax.psum_scatter(d_up, "seq", scatter_dimension=1, tiled=True),
        lax.psum_scatter(d_down, "seq", scatter_dimension=1, tiled=True),
    )
    mats_done = (
        lax.psum_scatter(mats_part[0], "batch", scatter_dimension=0, tiled=True),
        lax.psum_scatter(mats_part[1], "batch", scatter_dimension=0, tiled=True),
        lax.psum_scatter(mats_part[2], "batch", scatter_dimension=0, tiled=True),
        lax.psum_scatter(mats_part[3], "batch", scatter_dimension=0, tiled=True),
    )
    qkv_total, out_total, up_total, down_total = mats_done
    vectors = lax.psum(
        (
            d_query_bias,
            d_value_bias,
            d_out_bias,
            d_gain_one,
            d_shift_one,
            d_up_bias,
            d_down_bias,
            d_gain_two,
            d_shift_two,
        ),
        ("batch", "seq"),
    )
    return (
        outputs,
        d_inputs.reshape(rows, local_len, width),
        qkv_total,
        vectors[0],
        vectors[1],
        out_total,
        vectors[2],
        vectors[3],
        vectors[4],
        up_total,
        vectors[5],
        down_total,
        vectors[6],
        vectors[7],
        vectors[8],
    )


def solution(mesh):
    placed = (
        P("batch", "seq", None),
        P("batch", None),
        P(),
        P(),
        P(),
        P(),
        P(),
        P(),
        P(),
        P(),
        P(),
        P(),
        P(),
        P(),
        P(),
        P("batch", "seq", None),
    )
    return jax.shard_map(
        body,
        mesh=mesh,
        in_specs=placed,
        out_specs=(
            P("batch", "seq", None),
            P("batch", "seq", None),
            P("batch", "seq"),
            P(),
            P(),
            P("batch", "seq"),
            P(),
            P(),
            P(),
            P("batch", "seq"),
            P(),
            P("batch", "seq"),
            P(),
            P(),
            P(),
        ),
        check_vma=False,
    )
```

profile of v0, /device:TPU:0, one launch (start us, length us, event | category | flops | bytes accessed | tf_op | source)
XLA Modules:
  0.0 870.2 jit_solution(6326495366198733760)
XLA Ops:
  13.8 6.2 reshape.286
  20.0 8.8 %copy.104 = bf16[2,256,3,768]{1,0,2,3:T(2,128)(2,1)} copy(bf16[2,256,3,768]{3,2,1,0:T(4,128)(2,1)} %reshape.286) | data formatting | bytes 4718592 | tf_op jit(solution)/shard_map/reshape | solution.py:92
  33.3 29.2 %all-to-all-done = bf16[2,256,3,768]{1,0,2,3:T(2,128)(2,1)} async-done(((bf16[2,256,3,768]{1,0,2,3:T(2,128)(2,1)}), bf16[2,256,3,768]{1,0,2,3:T(2,128)(2,1)}, u32[]{:S(2)}, u32[]{:S(2)}) %all-to-all-start) | async-done | bytes 2359328 | tf_op jit(solution)/shard_map/all_to_all | solution.py:91
  76.3 48.8 %while.22 = (s32[]{:T(128)}, bf16[2,1024,3,64]{1,3,2,0:T(8,128)(2,1)}, f32[2,3,1024]{2,1,0:T(4,128)}, bf16[2,1024,3,64]{1,3,2,0:T(8,128)(2,1)}, s32[2,1024]{1,0:...) while((s32[]{:T(128)}, ...), condition=%wide.region_3.4_spmd, body=%wide.region_0.3_spmd.sunk | while | flops 844297216 | bytes 46787188 | solution.py:100
  76.9 8.2 fusion.117
  85.2 7.4 fusion.118
  93.2 7.5 fusion.119
  101.4 8.2 fusion.117
  109.6 7.4 fusion.118
  117.6 7.5 fusion.119
  140.3 7.4 all-to-all-done.1
  157.5 19.6 %multiply_convert_fusion.1 = (bf16[512,3072]{1,0:T(8,128)(2,1)S(1)}, f32[512,3072]{1,0:T(8,128)}, f32[512,3072]{1,0:T(8,128)}) fusion(f32[3072]{0:T(1024)S(1)} %copy-done.26, bf16[768,3072]{1,0:T(8,128)(2,1)} %param.29, f32[512,768]{1,0:T(8,128)S(1)} %get-tuple-element.249, f32[768]{0:T(1024)S(1)} %copy-done.30, f32[768]{0:T(1024)S(1)} %copy-done.24, ...), kind=kOutput, calls=%fused_computation.68 | convolution fusion | flops 2521694208 | bytes 22042624 | tf_op jit(solution)/shard_map/dot_general | solution.py:112
  183.3 9.8 %convert_reduce_fusion = (f32[3072]{0:T(1024)}, bf16[512,3072]{1,0:T(8,128)(2,1)}) fusion(f32[512,3072]{1,0:T(8,128)} %get-tuple-element.239, bf16[3072,768]{1,0:T(8,128)(2,1)S(1)} %bitcast.193, f32[512,768]{1,0:T(8,128)S(1)} %get-tuple-element.237, f32[512]{0:T(512)S(1)} %negate_multiply_fusion.2, f32[512,3072]{1,0:T(8,128)} %get-tuple-element.250, ...), kind=kOutput, calls=%fused_computation.66 | convolution fusion | flops 2443441152 | bytes 22046720 | tf_op jit(solution)/shard_map/to,io->ti/dot_general | solution.py:129
  213.8 7.6 all-to-all-done.2
  226.9 57.5 %while.23 = (s32[]{:T(128)}, bf16[2,1024,3,3,64]{1,4,3,2,0:T(8,128)(2,1)}, bf16[2,1024,3,64]{1,3,2,0:T(8,128)(2,1)}, s32[2,1024]{1,0:T(2,128)S(1)}, bf16[2,1024,...) while((s32[]{:T(128)}, ...), condition=%wide.region_14.15_spmd, body=%wide.region_12.14_spmd.sunk | while | flops 2066019328 | bytes 119119104 | solution.py:148
  231.4 7.2 multiply_reduce_fusion.6
  238.6 7.1 multiply_convert_fusion.3
  260.2 7.2 multiply_reduce_fusion.6
  267.4 7.0 multiply_convert_fusion.3
  284.4 8.7 %copy.113 = bf16[2,1024,3,192]{3,0,2,1:T(2,128)(2,1)} copy(bf16[2,1024,3,192]{1,3,2,0:T(8,128)(2,1)} %bitcast.33) | data formatting | bytes 4718592 | tf_op jit(solution)/shard_map/reshape | solution.py:150
  293.1 42.5 %all_to_all.60 = bf16[2,1024,3,192]{3,0,2,1:T(2,128)(2,1)} all-to-all(bf16[2,1024,3,192]{3,0,2,1:T(2,128)(2,1)} %copy.113), channel_id=1, replica_groups=mesh['batch'=8,'seq'=4] {'seq'}, dimensions={1} | all-to-all | bytes 4718592 | tf_op jit(solution)/shard_map/all_to_all | solution.py:149
  335.6 9.1 %copy.125 = bf16[2,4,256,3,192]{2,1,4,3,0:T(4,128)(2,1)} copy(bf16[2,4,256,3,192]{4,0,3,2,1:T(2,128)(2,1)} %bitcast.176) | data formatting | bytes 4718592 | tf_op jit(solution)/shard_map/all_to_all | solution.py:149
  356.2 10.3 %fusion.68 = f32[3072,768]{0,1:T(8,128)} fusion(bf16[512,3072]{1,0:T(8,128)(2,1)} %copy-done.14, f32[512,768]{1,0:T(8,128)} %copy-done.7, f32[512]{0:T(512)S(1)} %copy-done.22), kind=kOutput, calls=%fused_computation.126 | convolution fusion | flops 2416705536 | bytes 14157824 | tf_op jit(solution)/shard_map/ti,to->io/dot_general | solution.py:128
  367.3 9.4 %fusion.71 = f32[768,3072]{1,0:T(8,128)} fusion(bf16[512,3072]{1,0:T(8,128)(2,1)} %get-tuple-element.255, f32[512,768]{1,0:T(8,128)} %copy-done.12, f32[768]{0:T(1024)} %convert_element_type.101, f32[768]{0:T(1024)S(1)} %copy-done.25, f32[512]{0:T(512)S(1)} %copy-done.28, f32[512]{0:T(512)S(1)} %copy-done.20), kind=kOutput, calls=%fused_computation.129 | convolution fusion | flops 2417885184 | bytes 14166016 | tf_op jit(solution)/shard_map/ti,to->io/dot_general | solution.py:133
  379.2 41.3 %reduce-scatter.13.cloned.1.call-done = f32[768,576]{0,1:T(8,128)} async-done(((f32[768,2304]{0,1:T(8,128)}), f32[768,576]{0,1:T(8,128)}) %reduce-scatter.13.cloned.1.call-update) | async-done | bytes 1769488 | tf_op jit(solution)/shard_map/reduce_scatter | solution.py:164
  423.4 78.1 %reduce-scatter.21.cloned.1.call-done = f32[3072,192]{0,1:T(8,128)} async-done(((f32[3072,768]{0,1:T(8,128)}), f32[3072,192]{0,1:T(8,128)}) %reduce-scatter.21.cloned.1.call-update) | async-done | bytes 2359312 | tf_op jit(solution)/shard_map/reduce_scatter | solution.py:167
  501.6 80.8 %reduce-scatter.17.cloned.1.call-done = f32[768,768]{1,0:T(8,128)} async-done(((f32[768,3072]{1,0:T(8,128)}), f32[768,768]{1,0:T(8,128)}) %reduce-scatter.17.cloned.1.call-update) | async-done | bytes 2359312 | tf_op jit(solution)/shard_map/reduce_scatter | solution.py:166
  588.5 41.3 %all-reduce = (f32[768]{0:T(1024)}, f32[768]{0:T(1024)}, f32[768]{0:T(1024)}, f32[768]{0:T(1024)}, f32[768]{0:T(1024)}, /*index=5*/f32[3072]{0:T(1024)}, f32[768]{0:T(1024)}, f32[768]{0:T(1024)}, f32[768]{0:T(1024)}) all-reduce(f32[768]{0:T(1024)} %get-tuple-element.193, ...), channel_id=1, replica_groups=mesh['batch'=8,'seq'=4] {'batch','seq'}, use_global_device_ids=true, to_apply=%region_18.19 | all-reduce | flops 9216 | bytes 73728 | tf_op jit(solution)/shard_map/psum | solution.py:176
  635.2 13.6 %reduce-scatter.27.cloned.1.call-done = f32[96,192]{1,0:T(8,128)} async-done(((f32[768,192]{1,0:T(8,128)}), f32[96,192]{1,0:T(8,128)}) %reduce-scatter.27.cloned.1.call-update) | async-done | bytes 73744
  648.8 70.0 %reduce-scatter.25.cloned.1.call-done = f32[96,576]{1,0:T(8,128)} async-done(((f32[768,576]{1,0:T(8,128)}), f32[96,576]{1,0:T(8,128)}) %reduce-scatter.25.cloned.1.call-update) | async-done | bytes 221200
  718.8 72.0 %reduce-scatter.23.cloned.1.call-done = f32[384,192]{0,1:T(8,128)} async-done(((f32[3072,192]{0,1:T(8,128)}), f32[384,192]{0,1:T(8,128)}) %reduce-scatter.23.cloned.1.call-update) | async-done | bytes 294928 | tf_op jit(solution)/shard_map/reduce_scatter | solution.py:173
  790.7 72.1 %reduce-scatter.19.cloned.1.call-done = f32[96,768]{1,0:T(8,128)} async-done(((f32[768,768]{1,0:T(8,128)}), f32[96,768]{1,0:T(8,128)}) %reduce-scatter.19.cloned.1.call-update) | async-done | bytes 294928 | tf_op jit(solution)/shard_map/reduce_scatter | solution.py:172
  (185 shorter events, 142.4 us)
Async XLA Ops:
  28.8 33.7 %all-to-all-start = ((bf16[2,256,3,768]{1,0,2,3:T(2,128)(2,1)}), bf16[2,256,3,768]{1,0,2,3:T(2,128)(2,1)}, u32[]{:S(2)}, u32[]{:S(2)}) async-start(bf16[2,256,3,768]{1,0,2,3:T(2,128)(2,1)} %copy.104), calls=%async_computation | async-start | bytes 4718592 | tf_op jit(solution)/shard_map/all_to_all | solution.py:91
  85.2 8.0 copy-start.8
  109.6 8.0 copy-start.8
  125.1 11.9 %copy-start.29 = (bf16[3072]{0:T(1024)(128)(2,1)S(1)}, bf16[3072]{0:T(1024)(128)(2,1)}, u32[]{:S(2)}) copy-start(bf16[3072]{0:T(1024)(128)(2,1)} %param.30) | copy-start | bytes 18436
  128.7 19.0 %all-to-all-start.1 = ((bf16[2,1024,192]{2,0,1:T(2,128)(2,1)}), bf16[2,1024,192]{2,0,1:T(2,128)(2,1)}, u32[]{:S(2)}, u32[]{:S(2)}) async-start(bf16[2,1024,192]{2,0,1:T(2,128)(2,1)} %copy.107), calls=%async_computation.1 | async-start | bytes 2097152 | tf_op jit(solution)/shard_map/all_to_all | solution.py:102
  154.5 22.6 %slice-start = ((s8[4718592]{0:T(1024)(128)(4,1)}), s8[4194304]{0:T(1024)(128)(4,1)S(1)}, s32[]{:S(2)}) async-start(s8[4718592]{0:T(1024)(128)(4,1)} %bitcast.192), calls=%async_computation.20 | async-start | bytes 8388608
  157.1 41.7 %copy-start.12 = (f32[512,768]{1,0:T(8,128)}, f32[512,768]{1,0:T(8,128)S(1)}, u32[]{:S(2)}) copy-start(f32[512,768]{1,0:T(8,128)S(1)} %get-tuple-element.249) | copy-start | bytes 4718596
  157.1 41.6 %copy-start.19 = (f32[512]{0:T(512)}, f32[512]{0:T(512)S(1)}, u32[]{:S(2)}) copy-start(f32[512]{0:T(512)S(1)} %broadcast_multiply_fusion.1) | copy-start | bytes 6148
  157.5 41.3 %copy-start.27 = (f32[512]{0:T(512)}, f32[512]{0:T(512)S(1)}, u32[]{:S(2)}) copy-start(f32[512]{0:T(512)S(1)} %fusion.66) | copy-start | bytes 6148
  157.5 19.7 %copy-start.31 = (f32[768]{0:T(1024)S(1)}, f32[768]{0:T(1024)}, u32[]{:S(2)}) copy-start(f32[768]{0:T(1024)} %convert_element_type.105) | copy-start | bytes 9220
  157.5 19.7 %slice-start.1 = ((s8[4718592]{0:T(1024)(128)(4,1)}), s8[524288]{0:T(1024)(128)(4,1)S(1)}, s32[]{:S(2)}) async-start(s8[4718592]{0:T(1024)(128)(4,1)} %bitcast.192), calls=%async_computation.21 | async-start | bytes 1048576
  181.7 11.4 %slice-start.2 = ((s8[4718592]{0:T(1024)(128)(4,1)}), s8[4194304]{0:T(1024)(128)(4,1)S(1)}, s32[]{:S(2)}) async-start(s8[4718592]{0:T(1024)(128)(4,1)} %bitcast.194), calls=%async_computation.22 | async-start | bytes 8388608
  183.3 9.8 %copy-start.7 = (f32[512,768]{1,0:T(8,128)}, f32[512,768]{1,0:T(8,128)S(1)}, u32[]{:S(2)}) copy-start(f32[512,768]{1,0:T(8,128)S(1)} %get-tuple-element.237) | copy-start | bytes 4718596
  183.3 9.8 %copy-start.21 = (f32[512]{0:T(512)}, f32[512]{0:T(512)S(1)}, u32[]{:S(2)}) copy-start(f32[512]{0:T(512)S(1)} %negate_multiply_fusion.2) | copy-start | bytes 6148
  183.3 9.8 %slice-start.3 = ((s8[4718592]{0:T(1024)(128)(4,1)}), s8[524288]{0:T(1024)(128)(4,1)S(1)}, s32[]{:S(2)}) async-start(s8[4718592]{0:T(1024)(128)(4,1)} %bitcast.194), calls=%async_computation.23 | async-start | bytes 1048576
  199.5 10.2 %copy-start.17 = (f32[512]{0:T(512)}, f32[512]{0:T(512)S(1)}, u32[]{:S(2)}) copy-start(f32[512]{0:T(512)S(1)} %negate_multiply_fusion.1) | copy-start | bytes 6148
  205.4 15.9 %all-to-all-start.2 = ((bf16[2,256,768]{1,0,2:T(2,128)(2,1)}), bf16[2,256,768]{1,0,2:T(2,128)(2,1)}, u32[]{:S(2)}, u32[]{:S(2)}) async-start(bf16[2,256,768]{1,0,2:T(2,128)(2,1)} %copy.110), calls=%async_computation.2 | async-start | bytes 1572864 | tf_op jit(solution)/shard_map/all_to_all | solution.py:144
  209.6 167.3 %reduce-scatter.15.cloned.1.call-start = ((), (), s32[]{:S(2)}) async-start(), calls=%async_computation.13 | async-start | bytes 2949120 | tf_op jit(solution)/shard_map/reduce_scatter | solution.py:165
  213.7 206.7 %reduce-scatter.13.cloned.1.call-start = ((), (), s32[]{:S(2)}) async-start(), calls=%async_computation.12 | async-start | bytes 8847360 | tf_op jit(solution)/shard_map/reduce_scatter | solution.py:164
  238.5 7.1 copy-start.2
  249.7 4.8 copy-start.1
  267.4 7.0 copy-start.2
  278.4 4.8 copy-start.1
  355.6 145.9 %reduce-scatter.21.cloned.1.call-start = ((), (), s32[]{:S(2)}) async-start(), calls=%async_computation.16 | async-start | bytes 11796480 | tf_op jit(solution)/shard_map/reduce_scatter | solution.py:167
  366.6 215.8 %reduce-scatter.17.cloned.1.call-start = ((), (), s32[]{:S(2)}) async-start(), calls=%async_computation.14 | async-start | bytes 11796480 | tf_op jit(solution)/shard_map/reduce_scatter | solution.py:166
  376.8 272.0 %reduce-scatter.27.cloned.1.call-start = ((), (), s32[]{:S(2)}) async-start(), calls=%async_computation.19 | async-start | bytes 884736
  379.1 339.7 %reduce-scatter.25.cloned.1.call-start = ((), (), s32[]{:S(2)}) async-start(), calls=%async_computation.18 | async-start | bytes 2211840
  423.3 367.4 %reduce-scatter.23.cloned.1.call-start = ((), (), s32[]{:S(2)}) async-start(), calls=%async_computation.17 | async-start | bytes 2654208 | tf_op jit(solution)/shard_map/reduce_scatter | solution.py:173
  501.5 84.6 %copy-start.18 = (f32[512]{0:T(512)S(1)}, f32[512]{0:T(512)}, u32[]{:S(2)}) copy-start(f32[512]{0:T(512)} %copy-done.17) | copy-start | bytes 6148
  501.5 361.4 %reduce-scatter.19.cloned.1.call-start = ((), (), s32[]{:S(2)}) async-start(), calls=%async_computation.15 | async-start | bytes 2654208 | tf_op jit(solution)/shard_map/reduce_scatter | solution.py:172
  582.4 6.1 copy-start.23
  582.4 5.2 copy-start.5
  (22 other events, 53.3 us)
Sparse Core Ops, SparseCore 0:
  213.8 35.5 reduce-scatter.14
  355.7 64.6 reduce-scatter.12
  423.0 78.4 reduce-scatter.20
  503.9 78.4 reduce-scatter.16
  586.1 62.6 reduce-scatter.26
  653.1 65.6 reduce-scatter.24
  722.8 67.8 reduce-scatter.22
  794.8 68.0 reduce-scatter.18
where the time goes:
time: 882 us; the launch traced here: 870 us
  waiting for transfers between devices  472 us (54%)
  matrix products  150 us (17%)
  blocking collectives  83.8 us (10%)
  local copies, waits for them, and re-layouts  81 us (9%)
  other arithmetic  54.1 us (6%)
  between operations  15 us (2%)
  starting transfers between devices  13.5 us (2%)
    unnamed x10, waiting for transfers between devices  83.7 us
    reduce_scatter x1, waiting for transfers between devices, body(): lax.psum_scatter(d_up, 'seq', scatter_dimension=1, tiled=True)  80.8 us
    reduce_scatter x1, waiting for transfers between devices, body(): lax.psum_scatter(d_down, 'seq', scatter_dimension=1, tiled=True)  78.1 us
    reduce_scatter x1, waiting for transfers between devices, body(): lax.psum_scatter(mats_part[2], 'batch', scatter_dimension=0, tiled=True)  72.1 us
    reduce_scatter x1, waiting for transfers between devices, body(): lax.psum_scatter(mats_part[3], 'batch', scatter_dimension=0, tiled=True)  72 us
    all_to_all x1, blocking collectives, body(): lax.all_to_all(d_split.reshape(rows, full_len, 3, per_head * DH), 'seq',...  42.5 us
    psum x1, blocking collectives, body(): lax.psum((d_query_bias, d_value_bias, d_out_bias, d_gain_one, d_shift_one...  41.3 us
    reduce_scatter x1, waiting for transfers between devices, body(): lax.psum_scatter(d_qkv, 'seq', scatter_dimension=1, tiled=True)  41.3 us
  transfers between devices with their start and end apart: 11, of which 10 were waited for; matrix products, arithmetic and copies ran while one was open for 16% of the time, Pallas kernels for 0%

commit v1 on v0

--- a/solution.py
+++ b/solution.py
@@ -6,6 +6,29 @@
 DH = 64
 EPS = 1e-05
 NEG = -1000000000.0
+
+
+def in_blocks(x, dim, size):
+    lengths = x.shape
+    parts = x.reshape(*lengths[:dim], size, lengths[dim] // size, *lengths[dim + 1 :])
+    return jnp.moveaxis(parts, dim, 0)
+
+
+def in_order(blocks, dim):
+    shape = list(blocks.shape[1:])
+    shape[dim] *= blocks.shape[0]
+    return jnp.moveaxis(blocks, 0, dim).reshape(shape)
+
+
+def pairwise_exchange(x, axis, split_dim, concat_dim):
+    peers, index = (lax.axis_size(axis), lax.axis_index(axis))
+    parts = in_blocks(x, split_dim, peers)
+    outs = [parts[index]]
+    for turn in range(1, peers):
+        sent = parts[index ^ turn]
+        outs.append(lax.ppermute(sent, axis, [(i, i ^ turn) for i in range(peers)]))
+    parts = jnp.stack(outs)[index ^ jnp.arange(peers)]
+    return in_order(parts, concat_dim)
 
 
 def layer_norm(values, gain, shift):
@@ -88,9 +111,7 @@
     projected = (
         jnp.dot(flat_in, qkv_weight, preferred_element_type=jnp.float32) + qkv_shift
     ).astype(jnp.bfloat16)
-    heads_in = lax.all_to_all(
-        projected.reshape(rows, local_len, 3, width), "seq", split_axis=3, concat_axis=1, tiled=True
-    )
+    heads_in = pairwise_exchange(projected.reshape(rows, local_len, 3, width), "seq", 3, 1)
     full_len = heads_in.shape[1]
     per_head = heads_in.shape[3] // DH
     split = heads_in.reshape(rows, full_len, 3, per_head, DH)

time: 882 us -> 882 us (level)
    all_to_all x1 -> x0, waiting for transfers between devices: 29.2 us -> none  [body(): lax.all_to_all(projected.reshape(rows, local_len, 3, width), 'seq', split...]
    ppermute x0 -> x3, waiting for transfers between devices: none -> 24.5 us  [pairwise_exchange(): outs.append(lax.ppermute(sent, axis, [(i, i ^ turn) for i in range(peers)]))]
    reshape x3 -> x0, local copies, waits for them, and re-layouts: 20.5 us -> none  [the longest x2 15 us: body(): projected.reshape(rows, local_len, 3, width)]
    another operation x0 -> x7, local copies, waits for them, and re-layouts: none -> 19.4 us
  transfers between devices with their start and end apart: 11 -> 13, of which waited for: 10 -> 11; matrix products, arithmetic and copies ran while one was open for 16% -> 16% of each run, Pallas kernels for 0% -> 0%
where the time goes in v1:
time: 882 us; the launch traced here: 873 us
  waiting for transfers between devices  468 us (53%)
  matrix products  150 us (17%)
  local copies, waits for them, and re-layouts  87.5 us (10%)
  blocking collectives  83.7 us (9%)
  other arithmetic  57.3 us (6%)
  between operations  14.8 us (2%)
  starting transfers between devices  12 us (1%)
    unnamed x10, waiting for transfers between devices  83.7 us
    reduce_scatter x1, waiting for transfers between devices, body(): lax.psum_scatter(d_up, 'seq', scatter_dimension=1, tiled=True)  80.8 us
    reduce_scatter x1, waiting for transfers between devices, body(): lax.psum_scatter(d_down, 'seq', scatter_dimension=1, tiled=True)  78.1 us
    reduce_scatter x1, waiting for transfers between devices, body(): lax.psum_scatter(mats_part[2], 'batch', scatter_dimension=0, tiled=True)  72.3 us
    reduce_scatter x1, waiting for transfers between devices, body(): lax.psum_scatter(mats_part[3], 'batch', scatter_dimension=0, tiled=True)  72 us
    all_to_all x1, blocking collectives, body(): lax.all_to_all(d_split.reshape(rows, full_len, 3, per_head * DH), 'seq',...  42.5 us
    psum x1, blocking collectives, body(): lax.psum((d_query_bias, d_value_bias, d_out_bias, d_gain_one, d_shift_one...  41.3 us
    reduce_scatter x1, waiting for transfers between devices, body(): lax.psum_scatter(d_qkv, 'seq', scatter_dimension=1, tiled=True)  41.1 us
  transfers between devices with their start and end apart: 13, of which 11 were waited for; matrix products, arithmetic and copies ran while one was open for 16% of the time, Pallas kernels for 0%

profile of v1, /device:TPU:0, one launch (start us, length us, event | category | flops | bytes accessed | tf_op | source)
XLA Modules:
  0.0 873.1 jit_solution(4506528530854525369)
XLA Ops:
  18.0 6.0 reshape_reshape.6
  35.1 12.3 %collective-permute-done.1 = bf16[2,256,3,192]{1,3,2,0:T(8,128)(2,1)} collective-permute-done((bf16[2,256,3,192]{1,3,2,0:T(8,128)(2,1)}, bf16[2,256,3,192]{1,3,2,0:T(8,128)(2,1)}, u32[]{:S(2)}, u32[]{:S(2)}) %collective-permute-start.1) | collective-permute-done | bytes 589856 | tf_op jit(solution)/shard_map/ppermute | solution.py:29
  47.4 12.3 %collective-permute-done.2 = bf16[2,256,3,192]{1,3,2,0:T(8,128)(2,1)} collective-permute-done((bf16[2,256,3,192]{1,3,2,0:T(8,128)(2,1)}, bf16[2,256,3,192]{1,3,2,0:T(8,128)(2,1)}, u32[]{:S(2)}, u32[]{:S(2)}) %collective-permute-start.2) | collective-permute-done | bytes 589856 | tf_op jit(solution)/shard_map/ppermute | solution.py:29
  80.0 49.0 %while.22 = (s32[]{:T(128)}, bf16[2,1024,3,64]{1,3,2,0:T(8,128)(2,1)}, f32[2,3,1024]{2,1,0:T(4,128)}, bf16[2,1024,3,64]{1,3,2,0:T(8,128)(2,1)}, s32[2,1024]{1,0:...) while((s32[]{:T(128)}, ...), condition=%wide.region_3.4_spmd, body=%wide.region_0.3_spmd.sunk | while | flops 844297216 | bytes 46787188 | solution.py:121
  80.9 8.2 fusion.118
  89.1 7.4 fusion.119
  97.1 7.5 fusion.120
  105.3 8.2 fusion.118
  113.5 7.4 fusion.119
  121.5 7.5 fusion.120
  144.2 7.4 all-to-all-done
  161.5 19.7 %multiply_convert_fusion.1 = (bf16[512,3072]{1,0:T(8,128)(2,1)S(1)}, f32[512,3072]{1,0:T(8,128)}, f32[512,3072]{1,0:T(8,128)}) fusion(f32[3072]{0:T(1024)S(1)} %copy-done.26, bf16[768,3072]{1,0:T(8,128)(2,1)} %param.29, f32[512,768]{1,0:T(8,128)S(1)} %get-tuple-element.253, f32[768]{0:T(1024)S(1)} %copy-done.30, f32[768]{0:T(1024)S(1)} %copy-done.24, ...), kind=kOutput, calls=%fused_computation.69 | convolution fusion | flops 2521694208 | bytes 22042624 | tf_op jit(solution)/shard_map/dot_general | solution.py:133
  187.3 9.8 %convert_reduce_fusion = (f32[3072]{0:T(1024)}, bf16[512,3072]{1,0:T(8,128)(2,1)}) fusion(f32[512,3072]{1,0:T(8,128)} %get-tuple-element.239, bf16[3072,768]{1,0:T(8,128)(2,1)S(1)} %bitcast.211, f32[512,768]{1,0:T(8,128)S(1)} %get-tuple-element.237, f32[512]{0:T(512)S(1)} %negate_multiply_fusion.2, f32[512,3072]{1,0:T(8,128)} %get-tuple-element.254, ...), kind=kOutput, calls=%fused_computation.67 | convolution fusion | flops 2443441152 | bytes 22046720 | tf_op jit(solution)/shard_map/to,io->ti/dot_general | solution.py:150
  217.7 7.6 all-to-all-done.1
  230.7 57.5 %while.23 = (s32[]{:T(128)}, bf16[2,1024,3,3,64]{1,4,3,2,0:T(8,128)(2,1)}, bf16[2,1024,3,64]{1,3,2,0:T(8,128)(2,1)}, s32[2,1024]{1,0:T(2,128)S(1)}, bf16[2,1024,...) while((s32[]{:T(128)}, ...), condition=%wide.region_14.15_spmd, body=%wide.region_12.14_spmd.sunk | while | flops 2066019328 | bytes 119119104 | solution.py:169
  235.2 7.2 multiply_reduce_fusion.6
  242.4 7.1 multiply_convert_fusion.3
  264.0 7.2 multiply_reduce_fusion.6
  271.2 7.0 multiply_convert_fusion.3
  288.2 8.6 copy.124
  296.9 42.5 %all_to_all.45 = bf16[2,1024,3,192]{3,0,2,1:T(2,128)(2,1)} all-to-all(bf16[2,1024,3,192]{3,0,2,1:T(2,128)(2,1)} %copy.124), channel_id=1, replica_groups=mesh['batch'=8,'seq'=4] {'seq'}, dimensions={1} | all-to-all | bytes 4718592 | tf_op jit(solution)/shard_map/all_to_all | solution.py:170
  339.3 9.0 %copy.134 = bf16[2,4,256,3,192]{2,1,4,3,0:T(4,128)(2,1)} copy(bf16[2,4,256,3,192]{4,0,3,2,1:T(2,128)(2,1)} %bitcast.194) | data formatting | bytes 4718592 | tf_op jit(solution)/shard_map/all_to_all | solution.py:170
  360.0 9.7 %fusion.69 = f32[3072,768]{0,1:T(8,128)} fusion(bf16[512,3072]{1,0:T(8,128)(2,1)} %copy-done.14, f32[512,768]{1,0:T(8,128)} %copy-done.7, f32[512]{0:T(512)S(1)} %copy-done.22), kind=kOutput, calls=%fused_computation.139 | convolution fusion | flops 2416705536 | bytes 14157824 | tf_op jit(solution)/shard_map/ti,to->io/dot_general | solution.py:149
  370.5 9.4 %fusion.72 = f32[768,3072]{1,0:T(8,128)} fusion(bf16[512,3072]{1,0:T(8,128)(2,1)} %get-tuple-element.259, f32[512,768]{1,0:T(8,128)} %copy-done.12, f32[768]{0:T(1024)} %convert_element_type.101, f32[768]{0:T(1024)S(1)} %copy-done.25, f32[512]{0:T(512)S(1)} %copy-done.28, f32[512]{0:T(512)S(1)} %copy-done.20), kind=kOutput, calls=%fused_computation.142 | convolution fusion | flops 2417885184 | bytes 14166016 | tf_op jit(solution)/shard_map/ti,to->io/dot_general | solution.py:154
  382.3 41.1 %reduce-scatter.13.cloned.1.call-done = f32[768,576]{0,1:T(8,128)} async-done(((f32[768,2304]{0,1:T(8,128)}), f32[768,576]{0,1:T(8,128)}) %reduce-scatter.13.cloned.1.call-update) | async-done | bytes 1769488 | tf_op jit(solution)/shard_map/reduce_scatter | solution.py:185
  426.3 78.1 %reduce-scatter.21.cloned.1.call-done = f32[3072,192]{0,1:T(8,128)} async-done(((f32[3072,768]{0,1:T(8,128)}), f32[3072,192]{0,1:T(8,128)}) %reduce-scatter.21.cloned.1.call-update) | async-done | bytes 2359312 | tf_op jit(solution)/shard_map/reduce_scatter | solution.py:188
  504.6 80.8 %reduce-scatter.17.cloned.1.call-done = f32[768,768]{1,0:T(8,128)} async-done(((f32[768,3072]{1,0:T(8,128)}), f32[768,768]{1,0:T(8,128)}) %reduce-scatter.17.cloned.1.call-update) | async-done | bytes 2359312 | tf_op jit(solution)/shard_map/reduce_scatter | solution.py:187
  591.5 41.3 %all-reduce = (f32[768]{0:T(1024)}, f32[768]{0:T(1024)}, f32[768]{0:T(1024)}, f32[768]{0:T(1024)}, f32[768]{0:T(1024)}, /*index=5*/f32[3072]{0:T(1024)}, f32[768]{0:T(1024)}, f32[768]{0:T(1024)}, f32[768]{0:T(1024)}) all-reduce(f32[768]{0:T(1024)} %get-tuple-element.193, ...), channel_id=1, replica_groups=mesh['batch'=8,'seq'=4] {'batch','seq'}, use_global_device_ids=true, to_apply=%region_18.19 | all-reduce | flops 9216 | bytes 73728 | tf_op jit(solution)/shard_map/psum | solution.py:197
  638.1 13.7 %reduce-scatter.27.cloned.1.call-done = f32[96,192]{1,0:T(8,128)} async-done(((f32[768,192]{1,0:T(8,128)}), f32[96,192]{1,0:T(8,128)}) %reduce-scatter.27.cloned.1.call-update) | async-done | bytes 73744
  651.8 69.9 %reduce-scatter.25.cloned.1.call-done = f32[96,576]{1,0:T(8,128)} async-done(((f32[768,576]{1,0:T(8,128)}), f32[96,576]{1,0:T(8,128)}) %reduce-scatter.25.cloned.1.call-update) | async-done | bytes 221200
  721.7 72.0 %reduce-scatter.23.cloned.1.call-done = f32[384,192]{0,1:T(8,128)} async-done(((f32[3072,192]{0,1:T(8,128)}), f32[384,192]{0,1:T(8,128)}) %reduce-scatter.23.cloned.1.call-update) | async-done | bytes 294928 | tf_op jit(solution)/shard_map/reduce_scatter | solution.py:194
  793.7 72.3 %reduce-scatter.19.cloned.1.call-done = f32[96,768]{1,0:T(8,128)} async-done(((f32[768,768]{1,0:T(8,128)}), f32[96,768]{1,0:T(8,128)}) %reduce-scatter.19.cloned.1.call-update) | async-done | bytes 294928 | tf_op jit(solution)/shard_map/reduce_scatter | solution.py:193
  (197 shorter events, 159.7 us)
Async XLA Ops:
  29.1 6.1 collective-permute-start
  30.4 17.0 %collective-permute-start.1 = (bf16[2,256,3,192]{1,3,2,0:T(8,128)(2,1)}, bf16[2,256,3,192]{1,3,2,0:T(8,128)(2,1)}, u32[]{:S(2)}, u32[]{:S(2)}) collective-permute-start(bf16[2,256,3,192]{1,3,2,0:T(8,128)(2,1)} %bitcast.147), channel_id=1, source_target_pairs={{0,2},{1,3},{2,0},{3,1},{4,6},{5,7},{6,4},{7,5},{8,10},{9,11},{10,... | collective-permute-start | bytes 1769480 | tf_op jit(solution)/shard_map/ppermute | solution.py:29
  33.8 25.8 %collective-permute-start.2 = (bf16[2,256,3,192]{1,3,2,0:T(8,128)(2,1)}, bf16[2,256,3,192]{1,3,2,0:T(8,128)(2,1)}, u32[]{:S(2)}, u32[]{:S(2)}) collective-permute-start(bf16[2,256,3,192]{1,3,2,0:T(8,128)(2,1)} %bitcast.146), channel_id=1, source_target_pairs={{0,3},{1,2},{2,1},{3,0},{4,7},{5,6},{6,5},{7,4},{8,11},{9,10},{10,... | collective-permute-start | bytes 1769480 | tf_op jit(solution)/shard_map/ppermute | solution.py:29
  89.1 8.0 copy-start.8
  113.5 8.0 copy-start.8
  129.0 11.9 %copy-start.29 = (bf16[3072]{0:T(1024)(128)(2,1)S(1)}, bf16[3072]{0:T(1024)(128)(2,1)}, u32[]{:S(2)}) copy-start(bf16[3072]{0:T(1024)(128)(2,1)} %param.30) | copy-start | bytes 18436
  132.7 19.0 %all-to-all-start = ((bf16[2,1024,192]{2,0,1:T(2,128)(2,1)}), bf16[2,1024,192]{2,0,1:T(2,128)(2,1)}, u32[]{:S(2)}, u32[]{:S(2)}) async-start(bf16[2,1024,192]{2,0,1:T(2,128)(2,1)} %copy.118), calls=%async_computation | async-start | bytes 2097152 | tf_op jit(solution)/shard_map/all_to_all | solution.py:123
  158.5 22.7 %slice-start = ((s8[4718592]{0:T(1024)(128)(4,1)}), s8[4194304]{0:T(1024)(128)(4,1)S(1)}, s32[]{:S(2)}) async-start(s8[4718592]{0:T(1024)(128)(4,1)} %bitcast.210), calls=%async_computation.19 | async-start | bytes 8388608
  161.0 41.7 %copy-start.12 = (f32[512,768]{1,0:T(8,128)}, f32[512,768]{1,0:T(8,128)S(1)}, u32[]{:S(2)}) copy-start(f32[512,768]{1,0:T(8,128)S(1)} %get-tuple-element.253) | copy-start | bytes 4718596
  161.1 41.7 %copy-start.19 = (f32[512]{0:T(512)}, f32[512]{0:T(512)S(1)}, u32[]{:S(2)}) copy-start(f32[512]{0:T(512)S(1)} %broadcast_multiply_fusion.1) | copy-start | bytes 6148
  161.4 41.4 %copy-start.27 = (f32[512]{0:T(512)}, f32[512]{0:T(512)S(1)}, u32[]{:S(2)}) copy-start(f32[512]{0:T(512)S(1)} %fusion.66) | copy-start | bytes 6148
  161.4 19.7 %copy-start.31 = (f32[768]{0:T(1024)S(1)}, f32[768]{0:T(1024)}, u32[]{:S(2)}) copy-start(f32[768]{0:T(1024)} %convert_element_type.105) | copy-start | bytes 9220
  161.4 19.7 %slice-start.1 = ((s8[4718592]{0:T(1024)(128)(4,1)}), s8[524288]{0:T(1024)(128)(4,1)S(1)}, s32[]{:S(2)}) async-start(s8[4718592]{0:T(1024)(128)(4,1)} %bitcast.210), calls=%async_computation.20 | async-start | bytes 1048576
  185.6 11.4 %slice-start.2 = ((s8[4718592]{0:T(1024)(128)(4,1)}), s8[4194304]{0:T(1024)(128)(4,1)S(1)}, s32[]{:S(2)}) async-start(s8[4718592]{0:T(1024)(128)(4,1)} %bitcast.212), calls=%async_computation.21 | async-start | bytes 8388608
  187.3 9.8 %copy-start.7 = (f32[512,768]{1,0:T(8,128)}, f32[512,768]{1,0:T(8,128)S(1)}, u32[]{:S(2)}) copy-start(f32[512,768]{1,0:T(8,128)S(1)} %get-tuple-element.237) | copy-start | bytes 4718596
  187.3 9.8 %copy-start.21 = (f32[512]{0:T(512)}, f32[512]{0:T(512)S(1)}, u32[]{:S(2)}) copy-start(f32[512]{0:T(512)S(1)} %negate_multiply_fusion.2) | copy-start | bytes 6148
  187.3 9.8 %slice-start.3 = ((s8[4718592]{0:T(1024)(128)(4,1)}), s8[524288]{0:T(1024)(128)(4,1)S(1)}, s32[]{:S(2)}) async-start(s8[4718592]{0:T(1024)(128)(4,1)} %bitcast.212), calls=%async_computation.22 | async-start | bytes 1048576
  203.5 10.2 %copy-start.17 = (f32[512]{0:T(512)}, f32[512]{0:T(512)S(1)}, u32[]{:S(2)}) copy-start(f32[512]{0:T(512)S(1)} %negate_multiply_fusion.1) | copy-start | bytes 6148
  209.4 15.9 %all-to-all-start.1 = ((bf16[2,256,768]{1,0,2:T(2,128)(2,1)}), bf16[2,256,768]{1,0,2:T(2,128)(2,1)}, u32[]{:S(2)}, u32[]{:S(2)}) async-start(bf16[2,256,768]{1,0,2:T(2,128)(2,1)} %copy.121), calls=%async_computation.1 | async-start | bytes 1572864 | tf_op jit(solution)/shard_map/all_to_all | solution.py:165
  213.6 166.4 %reduce-scatter.15.cloned.1.call-start = ((), (), s32[]{:S(2)}) async-start(), calls=%async_computation.12 | async-start | bytes 2949120 | tf_op jit(solution)/shard_map/reduce_scatter | solution.py:186
  217.7 205.7 %reduce-scatter.13.cloned.1.call-start = ((), (), s32[]{:S(2)}) async-start(), calls=%async_computation.11 | async-start | bytes 8847360 | tf_op jit(solution)/shard_map/reduce_scatter | solution.py:185
  242.4 7.1 copy-start.2
  271.2 7.0 copy-start.2
  359.3 145.1 %reduce-scatter.21.cloned.1.call-start = ((), (), s32[]{:S(2)}) async-start(), calls=%async_computation.15 | async-start | bytes 11796480 | tf_op jit(solution)/shard_map/reduce_scatter | solution.py:188
  369.7 215.7 %reduce-scatter.17.cloned.1.call-start = ((), (), s32[]{:S(2)}) async-start(), calls=%async_computation.13 | async-start | bytes 11796480 | tf_op jit(solution)/shard_map/reduce_scatter | solution.py:187
  379.9 271.9 %reduce-scatter.27.cloned.1.call-start = ((), (), s32[]{:S(2)}) async-start(), calls=%async_computation.18 | async-start | bytes 884736
  382.2 339.5 %reduce-scatter.25.cloned.1.call-start = ((), (), s32[]{:S(2)}) async-start(), calls=%async_computation.17 | async-start | bytes 2211840
  426.3 367.4 %reduce-scatter.23.cloned.1.call-start = ((), (), s32[]{:S(2)}) async-start(), calls=%async_computation.16 | async-start | bytes 2654208 | tf_op jit(solution)/shard_map/reduce_scatter | solution.py:194
  504.5 84.5 %copy-start.18 = (f32[512]{0:T(512)S(1)}, f32[512]{0:T(512)}, u32[]{:S(2)}) copy-start(f32[512]{0:T(512)} %copy-done.17) | copy-start | bytes 6148
  504.5 361.5 %reduce-scatter.19.cloned.1.call-start = ((), (), s32[]{:S(2)}) async-start(), calls=%async_computation.14 | async-start | bytes 2654208 | tf_op jit(solution)/shard_map/reduce_scatter | solution.py:193
  585.4 6.1 copy-start.23
  585.4 5.2 copy-start.5
  (24 other events, 62.8 us)
Sparse Core Ops, SparseCore 0:
  217.8 34.7 reduce-scatter.14
  359.5 63.8 reduce-scatter.12
  426.0 78.4 reduce-scatter.20
  506.9 78.3 reduce-scatter.16
  589.1 62.6 reduce-scatter.26
  656.1 65.5 reduce-scatter.24
  725.8 67.8 reduce-scatter.22
  797.7 68.2 reduce-scatter.18
